TPU v7x, 32 devices: a whole 2x2x4 slice. The times are simulated.
32 devices in a mesh: grp: 2 (over x), res: 16 (over z, y, core).
Axes of the slice: x: 2, y: 2, z: 4, core: 2. Of those that a mesh axis runs over, the one named last changes fastest.
Arguments:
- alignment_activations: bfloat16 [128, 128, 256], P('grp', 'res'), parts along dimension 0, may hold values from -6 to 6
- projection_weight: bfloat16 [256, 64], replicated, may hold values from -0.375 to 0.375
- output_weight: bfloat16 [1024, 128], replicated, may hold values from -0.1875 to 0.1875
- output_bias: float32 [128], replicated, may hold values from -3 to 3
- pair_update_gradient: bfloat16 [256, 128, 128], P(('grp', 'res')), parts along dimension 0, may hold values from -6 to 6
- sequence_mask: int32 [128], P('grp'), parts along dimension 0, may hold values 0 or 1
- residue_mask: int32 [256], P('grp'), parts along dimension 0, may hold values 0 or 1
Outputs:
- pair_increment: bfloat16 [256, 128, 128], P(('grp', 'res')), parts along dimension 0
- alignment_gradient: bfloat16 [128, 128, 256], P('grp', 'res'), parts along dimension 0
There are 2 independent parts, one for each index of `grp`. A program takes and returns all parts, laid end to end along the dimension named above; an argument that names none is the same for every part. Nothing has to cross between parts.
All inputs are finite; a program needn't handle non-finite values.
Results may differ from a plain program's by a relative error of at most 0.007.
Values may be sent and summed in bfloat16 or wider, within the bound.
No kernel may reach another device: no remote copies, remote signals or barrier semaphores. Data moves between devices by JAX's collectives and lax.ppermute only.
A program may use at most 64 MiB of HBM per device.

v0:
```python
import jax
import jax.numpy as jnp
from jax import lax
from jax.sharding import PartitionSpec as P

eps_norm = 1e-05


def layer_norm_forward(values):
    mean_val = jnp.mean(values, axis=-1, keepdims=True)
    centered = values - mean_val
    inverse_deviation = lax.rsqrt(jnp.mean(centered * centered, axis=-1, keepdims=True) + eps_norm)
    return (centered * inverse_deviation, inverse_deviation)


def layer_norm_backward(grad_out, scaled_product, inverse_deviation):
    mean_grad = jnp.mean(grad_out, axis=-1, keepdims=True)
    mean_cross = jnp.mean(grad_out * scaled_product, axis=-1, keepdims=True)
    return inverse_deviation * (grad_out - mean_grad - scaled_product * mean_cross)


def body(
    alignment_activations,
    projection_weight,
    output_weight,
    output_bias,
    pair_update_gradient,
    sequence_mask,
    residue_mask,
):
    alignment_rows = alignment_activations.shape[0]
    local_rows = alignment_activations.shape[1]
    alignment_width = alignment_activations.shape[2]
    projected_width = projection_weight.shape[1] // 2
    pair_width = output_weight.shape[1]
    row_start = lax.axis_index("res") * local_rows
    residue_float_mask = residue_mask.astype(jnp.float32)
    local_residues = lax.dynamic_slice_in_dim(residue_float_mask, row_start, local_rows)
    alignment_mask = sequence_mask.astype(jnp.float32)[:, None] * local_residues[None, :]
    scaled_product, inverse_deviation = layer_norm_forward(
        alignment_activations.astype(jnp.float32)
    )
    normalized_input = scaled_product.astype(jnp.bfloat16)
    projected_rows = jnp.dot(
        normalized_input.reshape(-1, alignment_width),
        projection_weight,
        preferred_element_type=jnp.float32,
    )
    projected_rows = (
        projected_rows.reshape(alignment_rows, local_rows, 2 * projected_width)
        * alignment_mask[:, :, None]
    )
    projected_rows = projected_rows.astype(jnp.bfloat16)
    left_projected = projected_rows[:, :, :projected_width]
    right_proj = projected_rows[:, :, projected_width:]
    live_rows = jnp.sum(sequence_mask.astype(jnp.float32))
    right_all = lax.all_gather(right_proj, "res", axis=1, tiled=True)
    residue_count = right_all.shape[1]
    block_columns = 256 if residue_count % 256 == 0 else residue_count
    block_count = residue_count // block_columns
    count_rows = jnp.maximum(live_rows * local_residues[:, None] * residue_float_mask[None, :], 1.0)

    def pair_block(carry, block_id):
        pair_increment, left_gradient, gradient_pieces = carry
        column_offset = block_id * block_columns
        right_blk = lax.dynamic_slice_in_dim(right_all, column_offset, block_columns, 1)
        cot_blk = lax.dynamic_slice_in_dim(pair_update_gradient, column_offset, block_columns, 1)
        count_blk = lax.dynamic_slice_in_dim(count_rows, column_offset, block_columns, 1)
        outer = jnp.einsum(
            "sic,sjd->ijcd", left_projected, right_blk, preferred_element_type=jnp.float32
        )
        outer = outer.astype(jnp.bfloat16).reshape(-1, projected_width * projected_width)
        update = jnp.dot(outer, output_weight, preferred_element_type=jnp.float32)
        update = update.reshape(local_rows, block_columns, pair_width) + output_bias
        update = (update / count_blk[:, :, None]).astype(jnp.bfloat16)
        pair_increment = lax.dynamic_update_slice_in_dim(pair_increment, update, column_offset, 1)
        grad_outer = jnp.dot(
            cot_blk.reshape(-1, pair_width), output_weight.T, preferred_element_type=jnp.float32
        )
        grad_outer = (
            grad_outer.reshape(local_rows, block_columns, projected_width, projected_width)
            / count_blk[:, :, None, None]
        )
        grad_outer = grad_outer.astype(jnp.bfloat16)
        left_gradient = left_gradient + jnp.einsum(
            "ijcd,sjd->sic", grad_outer, right_blk, preferred_element_type=jnp.float32
        )
        gradient_piece = jnp.einsum(
            "ijcd,sic->jsd", grad_outer, left_projected, preferred_element_type=jnp.float32
        )
        gradient_pieces = lax.dynamic_update_slice_in_dim(
            gradient_pieces,
            gradient_piece.reshape(block_columns, alignment_rows * projected_width),
            column_offset,
            0,
        )
        return ((pair_increment, left_gradient, gradient_pieces), None)

    start_update = jnp.zeros((local_rows, residue_count, pair_width), jnp.bfloat16)
    initial_left = jnp.zeros((alignment_rows, local_rows, projected_width), jnp.float32)
    initial_pieces = jnp.zeros((residue_count, alignment_rows * projected_width), jnp.float32)
    (pair_increment, left_gradient, gradient_pieces), unused = lax.scan(
        pair_block, (start_update, initial_left, initial_pieces), jnp.arange(block_count)
    )
    gradient_total = lax.psum_scatter(gradient_pieces, "res", scatter_dimension=0, tiled=True)
    right_gradient = gradient_total.reshape(local_rows, alignment_rows, projected_width).transpose(
        1, 0, 2
    )
    projection_gradient = (
        jnp.concatenate([left_gradient, right_gradient], axis=-1) * alignment_mask[:, :, None]
    )
    projection_gradient = projection_gradient.astype(jnp.bfloat16)
    normalized_gradient = jnp.dot(
        projection_gradient.reshape(-1, 2 * projected_width),
        projection_weight.T,
        preferred_element_type=jnp.float32,
    )
    normalized_gradient = normalized_gradient.reshape(alignment_rows, local_rows, alignment_width)
    alignment_gradient = layer_norm_backward(
        normalized_gradient, scaled_product, inverse_deviation
    ).astype(jnp.bfloat16)
    return (pair_increment, alignment_gradient)


def solution(mesh):
    in_specs = (
        P("grp", "res", None),
        P(),
        P(),
        P(),
        P(("grp", "res"), None, None),
        P("grp"),
        P("grp"),
    )
    out_specs = (P(("grp", "res"), None, None), P("grp", "res", None))
    return jax.shard_map(body, mesh=mesh, in_specs=in_specs, out_specs=out_specs, check_vma=False)
```

profile of v0, /device:TPU:0, one launch (start us, length us, event | category | flops | bytes accessed | tf_op | source)
XLA Modules:
  0.0 89.6 jit_solution(17013610262894951195)
XLA Ops:
  7.2 1.3 %convert_reduce_fusion.1 = f32[]{:T(128)} fusion(s32[64]{0:T(128)} %param.12), kind=kLoop, calls=%fused_computation.46 | loop fusion | flops 127 | bytes 260 | tf_op jit(solution)/shard_map/reduce_sum | solution.py:56
  8.5 0.7 convert_element_type.41
  9.2 0.7 convert_element_type.42
  9.9 1.1 %convert_reduce_fusion = f32[64,8]{1,0:T(8,128)S(1)} fusion(bf16[64,8,256]{2,1,0:T(8,128)(2,1)} %param.7), kind=kLoop, calls=%fused_computation.15 | loop fusion | flops 261632 | bytes 264192 | tf_op jit(solution)/shard_map/reduce_sum | solution.py:10
  11.0 1.2 %fusion.23 = f32[64,8]{1,0:T(8,128)S(1)} fusion(bf16[64,8,256]{2,1,0:T(8,128)(2,1)} %param.7, f32[64,8]{1,0:T(8,128)S(1)} %broadcast_multiply_fusion.3), kind=kLoop, calls=%fused_computation.25 | loop fusion | flops 523776 | bytes 266240 | tf_op jit(solution)/shard_map/reduce_sum | solution.py:12
  12.2 0.7 broadcast_multiply_fusion.4
  13.0 0.6 copy-done.4
  13.6 1.3 %fusion.9 = bf16[64,8,64]{2,1,0:T(8,128)(2,1)S(1)} fusion(bf16[64,8,256]{2,1,0:T(8,128)(2,1)} %param.7, f32[64,8]{1,0:T(8,128)S(1)} %get-tuple-element.29, f32[64,8]{1,0:T(8,128)S(1)} %broadcast_multiply_fusion.3, f32[64,8]{1,0:T(8,128)S(1)} %get-tuple-element.40, bf16[256,64]{0,1:T(8,128)(2,1)} %param.8), kind=kOutput, calls=%fused_computation.11 | convolution fusion | flops 17367040 | bytes 366592 | tf_op jit(solution)/shard_map/dot_general | solution.py:44
  15.2 0.7 divide_convert_fusion
  15.9 0.8 fusion.4
  16.7 0.6 copy.30
  17.3 1.3 %copy.43 = f32[128,2048]{1,0:T(8,128)} copy(f32[128,2048]{0,1:T(8,128)S(1)} %bitcast.49) | data formatting | bytes 2097152
  18.7 32.3 %all_gather.3 = bf16[64,128,32]{2,1,0:T(8,128)(2,1)S(1)} all-gather(bf16[64,8,32]{2,1,0:T(8,128)(2,1)S(1)} %get-tuple-element.27), channel_id=1, replica_groups=mesh['grp'=2,'res'=16] {'res'}, dimensions={1}, use_global_device_ids=true | all-gather | bytes 557056 | tf_op jit(solution)/shard_map/all_gather | solution.py:57
  51.0 3.2 %copy.26 = bf16[64,128,32]{0,1,2:T(8,128)(2,1)S(1)} copy(bf16[64,128,32]{2,1,0:T(8,128)(2,1)S(1)} %all_gather.3) | data formatting | bytes 1048576 | tf_op jit(solution)/shard_map/all_gather | solution.py:57
  54.1 3.0 %fusion.10 = f32[64,8,32]{0,2,1:T(8,128)} fusion(bf16[8,128,32,32]{1,3,2,0:T(8,128)(2,1)} %copy-done.2, bf16[64,128,32]{0,1,2:T(8,128)(2,1)S(1)} %copy.26), kind=kOutput, calls=%fused_computation.12 | convolution fusion | flops 134217728 | bytes 2686976 | tf_op jit(solution)/shard_map/while/body/eval_jaxpr/ijcd,sjd->sic/dot_general | solution.py:85
  57.1 1.7 %copy.33 = f32[64,8,32]{2,1,0:T(8,128)} copy(f32[64,8,32]{0,2,1:T(8,128)} %fusion.10) | data formatting | bytes 131072 | tf_op jit(solution)/shard_map/while/body/eval_jaxpr/ijcd,sjd->sic/dot_general | solution.py:85
  58.9 3.2 %copy.34 = bf16[64,128,32,1]{0,1,3,2:T(8,128)(2,1)S(1)} copy(bf16[64,128,32,1]{2,1,0,3:T(8,128)(2,1)S(1)} %bitcast.47) | data formatting | bytes 1048576 | tf_op jit(solution)/shard_map/all_gather | solution.py:57
  62.1 0.7 convert_bitcast_fusion
  62.8 1.4 %copy.24 = bf16[8,128,32,32]{1,3,2,0:T(8,128)(2,1)S(1)} copy(bf16[8,128,32,32]{1,2,0,3:T(8,128)(2,1)S(1)} %convert_bitcast_fusion) | data formatting | bytes 4194304 | tf_op jit(solution)/shard_map/while/body/eval_jaxpr/convert_element_type | solution.py:72
  64.2 1.5 %fusion.8 = bf16[8,128,128]{2,1,0:T(8,128)(2,1)} fusion(bf16[8,128,1024]{1,2,0:T(8,128)(2,1)S(1)} %bitcast.50, bf16[1024,128]{1,0:T(8,128)(2,1)S(1)} %copy-done, f32[8,128]{1,0:T(8,128)S(1)} %multiply_maximum_fusion, f32[128]{0:T(128)S(1)} %copy-done.8), kind=kOutput, calls=%fused_computation.9 | convolution fusion | flops 268828672 | bytes 2626048 | tf_op jit(solution)/shard_map/while/body/eval_jaxpr/dot_general | solution.py:73
  65.7 14.0 %reduce-scatter.4.cloned.1.call-done = f32[8,2048]{1,0:T(8,128)} async-done(((f32[128,2048]{1,0:T(8,128)}), f32[8,2048]{1,0:T(8,128)}) %reduce-scatter.4.cloned.1.call-update) | async-done | bytes 65552
  79.7 1.2 %copy.44 = f32[8,2048]{0,1:T(8,128)S(1)} copy(f32[8,2048]{1,0:T(8,128)} %reduce-scatter.4.cloned.1.call-done) | data formatting | bytes 131072
  81.2 0.5 fusion.38
  81.8 1.0 %fusion.22 = bf16[64,8,256]{2,1,0:T(8,128)(2,1)} fusion(bf16[64,8,256]{2,1,0:T(8,128)(2,1)S(1)} %copy-done.1, f32[64,8,256]{2,1,0:T(8,128)S(1)} %get-tuple-element.28, f32[64,8]{1,0:T(8,128)S(1)} %broadcast_multiply_fusion.1, f32[64,8]{1,0:T(8,128)S(1)} %broadcast_multiply_fusion.2, f32[64,8]{1,0:T(8,128)S(1)} %get-tuple-element.29, ...), kind=kLoop, calls=%fused_computation.24 | loop fusion | flops 1048576 | bytes 1056768 | tf_op jit(solution)/shard_map/convert_element_type | solution.py:121
  (27 shorter events, 0.8 us)
Async XLA Ops:
  7.2 8.0 %copy-start = (bf16[1024,128]{1,0:T(8,128)(2,1)S(1)}, bf16[1024,128]{1,0:T(8,128)(2,1)}, u32[]{:S(2)}) copy-start(bf16[1024,128]{1,0:T(8,128)(2,1)} %param.9) | copy-start | bytes 786436
  7.2 8.0 %copy-start.7 = (bf16[8,128,128]{2,1,0:T(8,128)(2,1)S(1)}, bf16[8,128,128]{2,1,0:T(8,128)(2,1)}, u32[]{:S(2)}) copy-start(bf16[8,128,128]{2,1,0:T(8,128)(2,1)} %param.11) | copy-start | bytes 786436
  7.2 72.5 %reduce-scatter.4.cloned.1.call-start = ((), (), s32[]{:S(2)}) async-start(), calls=%async_computation.1 | async-start | bytes 1114112
  13.0 0.6 copy-start.4
  15.9 1.4 %copy-start.2 = (bf16[8,128,32,32]{1,3,2,0:T(8,128)(2,1)}, bf16[8,128,32,32]{1,3,2,0:T(8,128)(2,1)S(1)}, u32[]{:S(2)}) copy-start(bf16[8,128,32,32]{1,3,2,0:T(8,128)(2,1)S(1)} %divide_convert_fusion) | copy-start | bytes 6291460
  62.8 1.4 %copy-start.8 = (f32[128]{0:T(128)S(1)}, f32[128]{0:T(128)}, u32[]{:S(2)}) copy-start(f32[128]{0:T(128)} %param.10) | copy-start | bytes 1540
  65.6 15.5 %copy-start.1 = (bf16[64,8,256]{2,1,0:T(8,128)(2,1)S(1)}, bf16[64,8,256]{2,1,0:T(8,128)(2,1)}, u32[]{:S(2)}) copy-start(bf16[64,8,256]{2,1,0:T(8,128)(2,1)} %param.7) | copy-start | bytes 786436
  65.7 15.5 %copy-start.3 = (f32[64,8,32]{2,1,0:T(8,128)S(1)}, f32[64,8,32]{2,1,0:T(8,128)}, u32[]{:S(2)}) copy-start(f32[64,8,32]{2,1,0:T(8,128)} %copy.33) | copy-start | bytes 196612
  65.7 15.5 %copy-start.5 = (f32[64,8]{1,0:T(8,128)S(1)}, f32[64,8]{1,0:T(8,128)}, u32[]{:S(2)}) copy-start(f32[64,8]{1,0:T(8,128)} %copy-done.4) | copy-start | bytes 6148
  65.7 15.6 %copy-start.6 = (bf16[256,64]{0,1:T(8,128)(2,1)S(1)}, bf16[256,64]{0,1:T(8,128)(2,1)}, u32[]{:S(2)}) copy-start(bf16[256,64]{0,1:T(8,128)(2,1)} %param.8) | copy-start | bytes 98308
Sparse Core Ops, SparseCore 0:
  18.8 60.8 reduce-scatter.3
where the time goes:
time: 90 us; the launch traced here: 89.6 us
  blocking collectives  32.3 us (36%)
  between operations  14.2 us (16%)
  waiting for transfers between devices  14 us (16%)
  local copies, waits for them, and re-layouts  13.8 us (15%)
  matrix products  8.48 us (9%)
  other arithmetic  6.82 us (8%)
    all_gather x1, blocking collectives, body(): right_all = lax.all_gather(right_proj, 'res', axis=1, tiled=True)  32.3 us
    unnamed x2, waiting for transfers between devices  14 us
    all_gather x2, local copies, waits for them, and re-layouts, body(): right_all = lax.all_gather(right_proj, 'res', axis=1, tiled=True)  6.35 us
    unnamed x20, local copies, waits for them, and re-layouts  3.13 us
    dot_general x1, matrix products, pair_block(): jnp.einsum('ijcd,sjd->sic', grad_outer, right_blk, preferred_element_type...  2.99 us
  transfers between devices with their start and end apart: 1, of which 1 were waited for; matrix products, arithmetic and copies ran while one was open for 16% of the time, Pallas kernels for 0%

commit v1 on v0

--- a/solution.py
+++ b/solution.py
@@ -1,9 +1,42 @@
+import functools
 import jax
 import jax.numpy as jnp
 from jax import lax
 from jax.sharding import PartitionSpec as P
 
 eps_norm = 1e-05
+
+
+def set_positions(local_values, pos_dim):
+    e_next = list(local_values.shape[1:])
+    e_next[pos_dim] *= local_values.shape[0]
+    current_arr = jnp.moveaxis(local_values, 0, pos_dim).reshape(e_next)
+    return current_arr
+
+
+def attach_the_arrays(message, shard_axis):
+    block_last = jax.lax.axis_size(shard_axis)
+    odd = jax.lax.axis_index(shard_axis)
+    a_next, z2 = (block_last, odd)
+    o_now, mixed_arr = (message[None], 1)
+    while mixed_arr < a_next:
+        tmp = range(a_next)
+        local_out = list(map(lambda hop_no: (hop_no, hop_no ^ mixed_arr), tmp))
+        base_arr = jax.lax.ppermute(o_now, axis_name=shard_axis, perm=local_out)
+        back = z2 & mixed_arr == 0
+        ready = jnp.where(back, o_now, base_arr)
+        o_now = jnp.concatenate([ready, jnp.where(back, base_arr, o_now)])
+        mixed_arr *= 2
+    return o_now
+
+
+def meet_tails(xin, panel, ndim_at):
+    local_part = attach_the_arrays(xin, panel)
+    m_next = set_positions(local_part, ndim_at)
+    return m_next
+
+
+play_table_up = functools.partial(meet_tails, panel="res", ndim_at=1)
 
 
 def layer_norm_forward(values):
@@ -54,7 +87,7 @@
     left_projected = projected_rows[:, :, :projected_width]
     right_proj = projected_rows[:, :, projected_width:]
     live_rows = jnp.sum(sequence_mask.astype(jnp.float32))
-    right_all = lax.all_gather(right_proj, "res", axis=1, tiled=True)
+    right_all = play_table_up(right_proj)
     residue_count = right_all.shape[1]
     block_columns = 256 if residue_count % 256 == 0 else residue_count
     block_count = residue_count // block_columns

time: 90 us -> 114 us (1.27)
  waiting for transfers between devices: 14 us -> 64 us
  blocking collectives: 32.3 us -> 0 us
  starting transfers between devices: 0.04 us -> 7.98 us
  local copies, waits for them, and re-layouts: 13.8 us -> 8.91 us
  matrix products: 8.48 us -> 10.8 us
  other arithmetic: 6.82 us -> 8.18 us
    ppermute x0 -> x4, waiting for transfers between devices: none -> 34.7 us  [attach_the_arrays(): base_arr = jax.lax.ppermute(o_now, axis_name=shard_axis, perm=local_out)]
    all_gather x1 -> x0, blocking collectives: 32.3 us -> none  [body(): right_all = lax.all_gather(right_proj, 'res', axis=1, tiled=True)]
    unnamed x2, waiting for transfers between devices: 14 us -> 29.3 us
    ppermute x0 -> x4, starting transfers between devices: none -> 7.94 us  [attach_the_arrays(): base_arr = jax.lax.ppermute(o_now, axis_name=shard_axis, perm=local_out)]
    all_gather x2 -> x0, local copies, waits for them, and re-layouts: 6.35 us -> none  [body(): right_all = lax.all_gather(right_proj, 'res', axis=1, tiled=True)]
    dot_general x1, local copies, waits for them, and re-layouts: 1.74 us -> 0.15 us  [pair_block(): jnp.einsum('ijcd,sjd->sic', grad_outer, right_blk, preferred_element_type...]
    dot_general x1, matrix products: 0.81 us -> 2.38 us  [pair_block(): jnp.einsum('ijcd,sic->jsd', grad_outer, left_projected, preferred_element...]
    transpose x0 -> x1, local copies, waits for them, and re-layouts: none -> 1.38 us  [set_positions(): current_arr = jnp.moveaxis(local_values, 0, pos_dim).reshape(e_next)]
  transfers between devices with their start and end apart: 1 -> 5, of which waited for: 1 -> 5; matrix products, arithmetic and copies ran while one was open for 16% -> 14% of each run, Pallas kernels for 0% -> 0%
where the time goes in v1:
time: 114 us
  waiting for transfers between devices  64 us (56%)
  between operations  14.2 us (12%)
  matrix products  10.8 us (9%)
  local copies, waits for them, and re-layouts  8.91 us (8%)
  other arithmetic  8.18 us (7%)
  starting transfers between devices  7.98 us (7%)
    ppermute x4, waiting for transfers between devices, attach_the_arrays(): base_arr = jax.lax.ppermute(o_now, axis_name=shard_axis, perm=local_out)  34.7 us
    unnamed x2, waiting for transfers between devices  29.3 us
    ppermute x4, starting transfers between devices, attach_the_arrays(): base_arr = jax.lax.ppermute(o_now, axis_name=shard_axis, perm=local_out)  7.94 us
    unnamed x16, local copies, waits for them, and re-layouts  2.53 us
    dot_general x1, matrix products, pair_block(): jnp.einsum('ijcd,sic->jsd', grad_outer, left_projected, preferred_element...  2.38 us
    dot_general x1, matrix products, pair_block(): jnp.einsum('ijcd,sjd->sic', grad_outer, right_blk, preferred_element_type...  2.31 us
  transfers between devices with their start and end apart: 5, of which 5 were waited for; matrix products, arithmetic and copies ran while one was open for 14% of the time, Pallas kernels for 0%

profile of v1, /device:TPU:0, one launch (start us, length us, event | category | flops | bytes accessed | tf_op | source)
XLA Modules:
  0.0 114.1 jit_solution(9521382975421033482)
XLA Ops:
  7.2 1.3 %convert_reduce_fusion.1 = f32[]{:T(128)} fusion(s32[64]{0:T(128)} %param.12), kind=kLoop, calls=%fused_computation.60 | loop fusion | flops 127 | bytes 260 | tf_op jit(solution)/shard_map/reduce_sum | solution.py:89
  9.8 1.1 convert_reduce_fusion
  10.9 1.2 %fusion.23 = f32[64,8]{1,0:T(8,128)S(1)} fusion(bf16[64,8,256]{2,1,0:T(8,128)(2,1)} %param.7, f32[64,8]{1,0:T(8,128)S(1)} %broadcast_multiply_fusion.3), kind=kLoop, calls=%fused_computation.29 | loop fusion | flops 523776 | bytes 266240 | tf_op jit(solution)/shard_map/reduce_sum | solution.py:45
  12.1 0.7 broadcast_multiply_fusion.4
  12.9 1.3 %fusion.9 = bf16[64,8,64]{2,1,0:T(8,128)(2,1)S(1)} fusion(bf16[64,8,256]{2,1,0:T(8,128)(2,1)} %param.7, f32[64,8]{1,0:T(8,128)S(1)} %get-tuple-element.47, f32[64,8]{1,0:T(8,128)S(1)} %broadcast_multiply_fusion.3, f32[64,8]{1,0:T(8,128)S(1)} %get-tuple-element.48, bf16[256,64]{0,1:T(8,128)(2,1)} %param.8), kind=kOutput, calls=%fused_computation.12 | convolution fusion | flops 17367040 | bytes 366592 | tf_op jit(solution)/shard_map/dot_general | solution.py:77
  14.9 1.0 collective-permute-done
  16.1 2.9 %collective-permute-start.1 = (bf16[2,64,8,32]{3,2,1,0:T(8,128)(2,1)S(1)}, bf16[2,64,8,32]{3,2,1,0:T(8,128)(2,1)S(1)}, u32[]{:S(2)}, u32[]{:S(2)}) collective-permute-start(bf16[2,64,8,32]{3,2,1,0:T(8,128)(2,1)S(1)} %pad_maximum_fusion.2), channel_id=1, source_target_pairs={{0,2},{1,3},{2,0},{3,1},{4,6},{5,7},{6,4},{7,5},{8,10},{9,11},{10,... | collective-permute-start | bytes 196616 | tf_op jit(solution)/shard_map/ppermute | solution.py:25
  19.1 6.5 %collective-permute-done.1 = bf16[2,64,8,32]{3,2,1,0:T(8,128)(2,1)S(1)} collective-permute-done((bf16[2,64,8,32]{3,2,1,0:T(8,128)(2,1)S(1)}, bf16[2,64,8,32]{3,2,1,0:T(8,128)(2,1)S(1)}, u32[]{:S(2)}, u32[]{:S(2)}) %collective-permute-start.1) | collective-permute-done | bytes 65568 | tf_op jit(solution)/shard_map/ppermute | solution.py:25
  25.8 1.9 %collective-permute-start.2 = (bf16[4,64,8,32]{3,2,1,0:T(8,128)(2,1)S(1)}, bf16[4,64,8,32]{3,2,1,0:T(8,128)(2,1)S(1)}, u32[]{:S(2)}, u32[]{:S(2)}) collective-permute-start(bf16[4,64,8,32]{3,2,1,0:T(8,128)(2,1)S(1)} %pad_maximum_fusion.1), channel_id=1, source_target_pairs={{0,4},{1,5},{2,6},{3,7},{4,0},{5,1},{6,2},{7,3},{8,12},{9,13},{10,... | collective-permute-start | bytes 393224 | tf_op jit(solution)/shard_map/ppermute | solution.py:25
  27.7 2.0 %divide_convert_fusion = bf16[8,128,32,32]{1,3,2,0:T(8,128)(2,1)} fusion(bf16[32,32,128,1]{2,1,0,3:T(8,128)(2,1)S(1)} %bitcast.55, f32[8,128]{1,0:T(8,128)S(1)} %multiply_maximum_fusion, bf16[8,128,128]{2,1,0:T(8,128)(2,1)S(1)} %copy-done.5), kind=kOutput, calls=%fused_computation | convolution fusion | flops 270532608 | bytes 2625536 | tf_op jit(solution)/shard_map/while/body/eval_jaxpr/dot_general | solution.py:110
  29.8 9.4 %collective-permute-done.2 = bf16[4,64,8,32]{3,2,1,0:T(8,128)(2,1)S(1)} collective-permute-done((bf16[4,64,8,32]{3,2,1,0:T(8,128)(2,1)S(1)}, bf16[4,64,8,32]{3,2,1,0:T(8,128)(2,1)S(1)}, u32[]{:S(2)}, u32[]{:S(2)}) %collective-permute-start.2) | collective-permute-done | bytes 131104 | tf_op jit(solution)/shard_map/ppermute | solution.py:25
  40.3 2.6 %collective-permute-start.3 = (bf16[8,64,8,32]{1,3,2,0:T(8,128)(2,1)S(1)}, bf16[8,64,8,32]{1,3,2,0:T(8,128)(2,1)S(1)}, u32[]{:S(2)}, u32[]{:S(2)}) collective-permute-start(bf16[8,64,8,32]{1,3,2,0:T(8,128)(2,1)S(1)} %copy.22), channel_id=1, source_target_pairs={{0,8},{1,9},{2,10},{3,11},{4,12},{5,13},{6,14},{7,15},{8,0},{9,1},... | collective-permute-start | bytes 786440 | tf_op jit(solution)/shard_map/ppermute | solution.py:25
  42.9 2.4 %fusion.4 = f32[128,64,32]{0,1,2:T(8,128)S(1)} fusion(bf16[8,128,32,32]{1,3,2,0:T(8,128)(2,1)} %divide_convert_fusion, bf16[64,8,32]{0,2,1:T(8,128)(2,1)S(1)} %copy.27), kind=kOutput, calls=%fused_computation.7 | convolution fusion | flops 134217728 | bytes 3178496 | tf_op jit(solution)/shard_map/while/body/eval_jaxpr/ijcd,sic->jsd/dot_general | solution.py:121
  45.9 1.3 %copy.47 = f32[128,2048]{1,0:T(8,128)} copy(f32[128,2048]{0,1:T(8,128)S(1)} %bitcast.59) | data formatting | bytes 2097152
  47.2 17.8 %collective-permute-done.3 = bf16[8,64,8,32]{1,3,2,0:T(8,128)(2,1)S(1)} collective-permute-done((bf16[8,64,8,32]{1,3,2,0:T(8,128)(2,1)S(1)}, bf16[8,64,8,32]{1,3,2,0:T(8,128)(2,1)S(1)}, u32[]{:S(2)}, u32[]{:S(2)}) %collective-permute-start.3) | collective-permute-done | bytes 262176 | tf_op jit(solution)/shard_map/ppermute | solution.py:25
  66.3 1.4 %copy.25 = bf16[64,16,8,32]{0,3,2,1:T(8,128)(2,1)S(1)} copy(bf16[64,16,8,32]{3,2,0,1:T(8,128)(2,1)S(1)} %maximum_bitcast_fusion) | data formatting | bytes 1048576 | tf_op jit(solution)/shard_map/transpose | solution.py:13
  67.7 1.1 copy.30
  68.8 2.3 %fusion.10 = f32[64,8,32]{0,2,1:T(8,128)S(1)} fusion(bf16[8,128,32,32]{1,3,2,0:T(8,128)(2,1)} %divide_convert_fusion, bf16[64,128,32]{1,0,2:T(8,128)(2,1)S(1)} %copy.30), kind=kOutput, calls=%fused_computation.13 | convolution fusion | flops 134217728 | bytes 2686976 | tf_op jit(solution)/shard_map/while/body/eval_jaxpr/ijcd,sjd->sic/dot_general | solution.py:118
  71.3 0.7 convert_bitcast_fusion
  72.0 1.4 %copy.28 = bf16[8,128,32,32]{1,3,2,0:T(8,128)(2,1)S(1)} copy(bf16[8,128,32,32]{1,2,0,3:T(8,128)(2,1)S(1)} %convert_bitcast_fusion) | data formatting | bytes 4194304 | tf_op jit(solution)/shard_map/while/body/eval_jaxpr/convert_element_type | solution.py:105
  73.4 1.5 %fusion.8 = bf16[8,128,128]{2,1,0:T(8,128)(2,1)} fusion(bf16[8,128,1024]{1,2,0:T(8,128)(2,1)S(1)} %bitcast.60, bf16[1024,128]{1,0:T(8,128)(2,1)S(1)} %copy-done, f32[8,128]{1,0:T(8,128)S(1)} %multiply_maximum_fusion, f32[128]{0:T(128)S(1)} %copy-done.6), kind=kOutput, calls=%fused_computation.10 | convolution fusion | flops 268828672 | bytes 2626048 | tf_op jit(solution)/shard_map/while/body/eval_jaxpr/dot_general | solution.py:106
  74.9 29.3 %reduce-scatter.4.cloned.1.call-done = f32[8,2048]{1,0:T(8,128)} async-done(((f32[128,2048]{1,0:T(8,128)}), f32[8,2048]{1,0:T(8,128)}) %reduce-scatter.4.cloned.1.call-update) | async-done | bytes 65552
  104.2 1.2 %copy.48 = f32[8,2048]{0,1:T(8,128)S(1)} copy(f32[8,2048]{1,0:T(8,128)} %reduce-scatter.4.cloned.1.call-done) | data formatting | bytes 131072
  106.2 1.0 fusion.22
  (40 shorter events, 6.5 us)
Async XLA Ops:
  7.2 20.5 %copy-start = (bf16[1024,128]{1,0:T(8,128)(2,1)S(1)}, bf16[1024,128]{1,0:T(8,128)(2,1)}, u32[]{:S(2)}) copy-start(bf16[1024,128]{1,0:T(8,128)(2,1)} %param.9) | copy-start | bytes 786436
  7.2 97.0 %reduce-scatter.4.cloned.1.call-start = ((), (), s32[]{:S(2)}) async-start(), calls=%async_computation.1 | async-start | bytes 1114112
  12.9 2.0 %copy-start.2 = (f32[64,8]{1,0:T(8,128)}, f32[64,8]{1,0:T(8,128)S(1)}, u32[]{:S(2)}) copy-start(f32[64,8]{1,0:T(8,128)S(1)} %get-tuple-element.48) | copy-start | bytes 6148
  14.2 13.4 %copy-start.5 = (bf16[8,128,128]{2,1,0:T(8,128)(2,1)S(1)}, bf16[8,128,128]{2,1,0:T(8,128)(2,1)}, u32[]{:S(2)}) copy-start(bf16[8,128,128]{2,1,0:T(8,128)(2,1)} %param.11) | copy-start | bytes 786436
  14.3 1.5 %collective-permute-start = (bf16[1,64,8,32]{3,2,1,0:T(8,128)(2,1)S(1)}, bf16[1,64,8,32]{3,2,1,0:T(8,128)(2,1)S(1)}, u32[]{:S(2)}, u32[]{:S(2)}) collective-permute-start(bf16[1,64,8,32]{3,2,1,0:T(8,128)(2,1)S(1)} %get-tuple-element.45), channel_id=1, source_target_pairs={{0,1},{1,0},{2,3},{3,2},{4,5},{5,4},{6,7},{7,6},{8,9},{9,8},{10,11... | collective-permute-start | bytes 98312 | tf_op jit(solution)/shard_map/ppermute | solution.py:25
  16.1 9.5 %collective-permute-start.1 = (bf16[2,64,8,32]{3,2,1,0:T(8,128)(2,1)S(1)}, bf16[2,64,8,32]{3,2,1,0:T(8,128)(2,1)S(1)}, u32[]{:S(2)}, u32[]{:S(2)}) collective-permute-start(bf16[2,64,8,32]{3,2,1,0:T(8,128)(2,1)S(1)} %pad_maximum_fusion.2), channel_id=1, source_target_pairs={{0,2},{1,3},{2,0},{3,1},{4,6},{5,7},{6,4},{7,5},{8,10},{9,11},{10,... | collective-permute-start | bytes 196616 | tf_op jit(solution)/shard_map/ppermute | solution.py:25
  25.8 13.5 %collective-permute-start.2 = (bf16[4,64,8,32]{3,2,1,0:T(8,128)(2,1)S(1)}, bf16[4,64,8,32]{3,2,1,0:T(8,128)(2,1)S(1)}, u32[]{:S(2)}, u32[]{:S(2)}) collective-permute-start(bf16[4,64,8,32]{3,2,1,0:T(8,128)(2,1)S(1)} %pad_maximum_fusion.1), channel_id=1, source_target_pairs={{0,4},{1,5},{2,6},{3,7},{4,0},{5,1},{6,2},{7,3},{8,12},{9,13},{10,... | collective-permute-start | bytes 393224 | tf_op jit(solution)/shard_map/ppermute | solution.py:25
  40.3 24.7 %collective-permute-start.3 = (bf16[8,64,8,32]{1,3,2,0:T(8,128)(2,1)S(1)}, bf16[8,64,8,32]{1,3,2,0:T(8,128)(2,1)S(1)}, u32[]{:S(2)}, u32[]{:S(2)}) collective-permute-start(bf16[8,64,8,32]{1,3,2,0:T(8,128)(2,1)S(1)} %copy.22), channel_id=1, source_target_pairs={{0,8},{1,9},{2,10},{3,11},{4,12},{5,13},{6,14},{7,15},{8,0},{9,1},... | collective-permute-start | bytes 786440 | tf_op jit(solution)/shard_map/ppermute | solution.py:25
  72.0 1.4 %copy-start.6 = (f32[128]{0:T(128)S(1)}, f32[128]{0:T(128)}, u32[]{:S(2)}) copy-start(f32[128]{0:T(128)} %param.10) | copy-start | bytes 1540
  74.9 30.8 %copy-start.1 = (bf16[64,8,256]{2,1,0:T(8,128)(2,1)S(1)}, bf16[64,8,256]{2,1,0:T(8,128)(2,1)}, u32[]{:S(2)}) copy-start(bf16[64,8,256]{2,1,0:T(8,128)(2,1)} %param.7) | copy-start | bytes 786436
  74.9 30.8 %copy-start.3 = (f32[64,8]{1,0:T(8,128)S(1)}, f32[64,8]{1,0:T(8,128)}, u32[]{:S(2)}) copy-start(f32[64,8]{1,0:T(8,128)} %copy-done.2) | copy-start | bytes 6148
  74.9 30.8 %copy-start.4 = (bf16[256,64]{0,1:T(8,128)(2,1)S(1)}, bf16[256,64]{0,1:T(8,128)(2,1)}, u32[]{:S(2)}) copy-start(bf16[256,64]{0,1:T(8,128)(2,1)} %param.8) | copy-start | bytes 98308
Sparse Core Ops, SparseCore 0:
  47.3 56.7 reduce-scatter.3
